TPU v7x, 256 devices: a whole 4x4x8 slice. The times are simulated.
256 devices in a mesh: dp: 16 (over x_lo, z), tensor: 16 (over y, x_hi, core).
Axes of the slice: x: 4 (x_hi: 2, x_lo: 2; x = x_hi * 2 + x_lo), y: 4, z: 8, core: 2. Of those that a mesh axis runs over, the one named last changes fastest.
Arguments:
- query_rows: bfloat16 [32768, 8192], P('dp', 'tensor'), may hold values from -16 to 16
- key_rows: bfloat16 [32768, 1024], P('dp'), may hold values from -10 to 10
- value_rows: bfloat16 [32768, 1024], P('dp'), may hold values from -600 to 600
- segment_ids: int32 [32768], P('dp'), may hold values from 0 to 127, never falling along the last dimension, each value on 1 to 512 neighbouring positions
- norm_gain: float32 [8192], replicated, may hold values from 0.1 to 1.9
- draft_weight: bfloat16 [8192, 512], P('tensor', 'dp'), may hold values from -0.0625 to 0.0625
- targets: bfloat16 [32768, 512], P(('dp', 'tensor')), may hold values from -6 to 6
Outputs:
- grad_weight: float32 [8192, 512], P('tensor', 'dp')
Inputs may be any that keep to these rules, and one draw needn't show every extreme that they name: `segment_ids`: document ids never fall along the tokens; a document has at most 512 tokens, and one has exactly 512.
All inputs are finite; a program needn't handle non-finite values.
Results may differ from a plain program's by a relative error of at most 0.0015.
Values may be sent and summed in bfloat16 or wider, within the bound.
No kernel may reach another device: no remote copies, remote signals or barrier semaphores. Data moves between devices by JAX's collectives and lax.ppermute only.
A program may use at most 128 MiB of HBM per device.

v0:
```python
import jax
import jax.numpy as jnp
from jax import lax
from jax.sharding import PartitionSpec as P

HEADS = 64
KV_HEADS = 8
HEAD_DIM = 128


def attend_local(query_rows, key_rows, value_rows, segment_ids):
    length = query_rows.shape[0]
    local_heads = query_rows.shape[1] // HEAD_DIM
    group = HEADS // KV_HEADS
    head_count = max(1, local_heads // group)
    repeats = local_heads // head_count
    first = lax.axis_index("tensor") * local_heads // group
    keys_local = lax.dynamic_slice_in_dim(
        key_rows, first * HEAD_DIM, head_count * HEAD_DIM, 1
    ).reshape(length, head_count, HEAD_DIM)
    values_local = lax.dynamic_slice_in_dim(
        value_rows, first * HEAD_DIM, head_count * HEAD_DIM, 1
    ).reshape(length, head_count, HEAD_DIM)
    grouped = query_rows.reshape(length, head_count, repeats, HEAD_DIM)
    width = min(length, 512)
    scale = HEAD_DIM ** (-0.5)
    places = jnp.arange(length, dtype=jnp.int32)

    def one_block(number):
        offset = number * width
        query_block = lax.dynamic_slice_in_dim(grouped, offset, width, 0)
        block_segments = lax.dynamic_slice_in_dim(segment_ids, offset, width, 0)
        block_places = offset + jnp.arange(width, dtype=jnp.int32)
        allowed = (block_segments[:, None] == segment_ids[None, :]) & (
            block_places[:, None] >= places[None, :]
        )
        scores = (
            jnp.einsum(
                "qgrd,kgd->grqk", query_block, keys_local, preferred_element_type=jnp.float32
            )
            * scale
        )
        scores = jnp.where(allowed[None, None], scores, -1e30)
        shifted = jnp.exp(scores - jnp.max(scores, axis=-1, keepdims=True))
        probs = (shifted / jnp.sum(shifted, axis=-1, keepdims=True)).astype(jnp.bfloat16)
        mixed = jnp.einsum(
            "grqk,kgd->qgrd", probs, values_local, preferred_element_type=jnp.float32
        )
        return mixed.astype(jnp.bfloat16).reshape(width, local_heads * HEAD_DIM)

    outputs = lax.map(one_block, jnp.arange(length // width, dtype=jnp.int32))
    return outputs.reshape(length, local_heads * HEAD_DIM)


def loss_derivative(predicted, targets, total_tokens):
    residual = predicted - targets.astype(jnp.float32)
    return (jnp.clip(residual, -1.0, 1.0) / jnp.sqrt(jnp.float32(total_tokens))).astype(
        jnp.bfloat16
    )


def on_device(query_rows, key_rows, value_rows, segment_ids, norm_gain, draft_weight, targets):
    attended = attend_local(query_rows, key_rows, value_rows, segment_ids)
    length = query_rows.shape[0]
    total_tokens = length * lax.axis_size("dp")
    weight_slab = lax.all_gather(draft_weight, "dp", axis=1, tiled=True)
    regrouped = lax.all_to_all(attended, "tensor", split_axis=0, concat_axis=1, tiled=True)
    features = regrouped.astype(jnp.float32)
    mean_square = jnp.mean(features * features, axis=-1, keepdims=True)
    normed = (features * lax.rsqrt(mean_square + 1e-06) * norm_gain[None, :]).astype(jnp.bfloat16)
    picked = normed
    predicted = jnp.dot(
        picked,
        lax.all_gather(weight_slab, "tensor", axis=0, tiled=True),
        preferred_element_type=jnp.float32,
    )
    grad_pred = loss_derivative(predicted, targets, total_tokens)
    picked = normed
    grad_slab = lax.psum_scatter(
        lax.dot_general(
            picked, grad_pred, (((0,), (0,)), ((), ())), preferred_element_type=jnp.float32
        ),
        "tensor",
        scatter_dimension=0,
        tiled=True,
    )
    return lax.psum_scatter(grad_slab, "dp", scatter_dimension=1, tiled=True)


def solution(mesh):
    placed = (
        P("dp", "tensor"),
        P("dp", None),
        P("dp", None),
        P("dp"),
        P(),
        P("tensor", "dp"),
        P(("dp", "tensor"), None),
    )
    return jax.shard_map(
        on_device, mesh=mesh, in_specs=placed, out_specs=P("tensor", "dp"), check_vma=False
    )
```

profile of v0, /device:TPU:8, one launch (start us, length us, event | category | flops | bytes accessed | tf_op | source)
XLA Modules:
  0.0 414.3 jit_solution(10289684197386694751)
XLA Ops:
  6.5 41.8 %all_gather.6 = bf16[512,512]{0,1:T(8,128)(2,1)} all-gather(bf16[512,32]{0,1:T(8,128)(2,1)} %param.14), channel_id=1, replica_groups=mesh['dp'=16,'tensor'=16] {'dp'}, dimensions={1}, use_global_device_ids=true | all-gather | bytes 557056 | tf_op jit(solution)/shard_map/all_gather | solution.py:66
  48.5 1.1 constant_dynamic-slice_fusion
  49.5 0.2 copy.17
  49.8 1.1 dynamic-slice_bitcast_fusion
  50.9 2.5 copy.16
  53.4 73.3 %while.11 = (s32[]{:T(128)}, bf16[4,512,512]{2,1,0:T(8,128)(2,1)}, s32[4]{0:T(128)S(1)}, s32[2048]{0:T(1024)S(1)}, bf16[2048,1,4,128]{0,3,2,1:T(8,128)(2,1)}, /*...) while((s32[]{:T(128)}, bf16[4,512,512]{2,1,0:T(8,128)(2,1)}, ...), condition=%wide.region_3.4_spmd.clone, body=%wide.region_0.3_spmd.clone.sunk | while | flops 2201219584 | bytes 58780336 | solution.py:51
  53.4 0.6 dynamic_slice.33
  54.7 0.1 dynamic_slice.34
  54.8 1.2 fusion.37
  56.0 4.9 %fusion.38 = (f32[4,512]{1,0:T(4,128)S(1)}, f32[512,4,2048]{2,0,1:T(8,128)S(1)}) fusion(pred[512,2048]{1,0:T(8,128)(4,1)S(1)} %fusion.37, bf16[2048,1,128]{2,0,1:T(8,128)(2,1)S(1)} %get-tuple-element.168, bf16[2048,1,4,128]{0,3,2,1:T(8,128)(2,1)} %get-tuple-element.167, s32[]{:T(128)S(6)} %select_n.40), kind=kOutput, calls=%fused_computation.5.clone.1 | convolution fusion | flops 1086322688 | bytes 18882564 | tf_op jit(solution)/shard_map/while/body/eval_jaxpr/qgrd,kgd->grqk/dot_general | solution.py:38
  60.9 4.5 %fusion.39 = f32[4,512]{1,0:T(4,128)S(1)} fusion(f32[512,4,2048]{2,0,1:T(8,128)S(1)} %get-tuple-element.139, f32[4,512]{1,0:T(4,128)S(1)} %get-tuple-element.140, pred[512,2048]{1,0:T(8,128)(4,1)S(1)} %fusion.37), kind=kLoop, calls=%fused_computation.4.clone.1 | loop fusion | flops 16775168 | bytes 17842176 | tf_op jit(solution)/shard_map/while/body/eval_jaxpr/reduce_sum | solution.py:45
  65.4 5.3 %fusion.40 = bf16[4,512,128]{1,2,0:T(8,128)(2,1)S(1)} fusion(f32[4,512]{1,0:T(4,128)S(1)} %fusion.39, f32[4,512]{1,0:T(4,128)S(1)} %get-tuple-element.140, f32[512,4,2048]{2,0,1:T(8,128)S(1)} %get-tuple-element.139, pred[512,2048]{1,0:T(8,128)(4,1)S(1)} %fusion.37, bf16[2048,1,128]{0,2,1:T(8,128)(2,1)S(1)} %get-tuple-element.169), kind=kOutput, calls=%fused_computation.10.clone.1 | convolution fusion | flops 1094975488 | bytes 18890752 | tf_op jit(solution)/shard_map/while/body/eval_jaxpr/grqk,kgd->qgrd/dot_general | solution.py:46
  70.7 0.2 copy.28
  70.9 0.9 constant_dynamic-update-slice_fusion.2
  71.7 0.6 dynamic_slice.33
  73.1 0.1 dynamic_slice.34
  73.2 1.2 fusion.37
  74.4 4.9 %fusion.38 = (f32[4,512]{1,0:T(4,128)S(1)}, f32[512,4,2048]{2,0,1:T(8,128)S(1)}) fusion(pred[512,2048]{1,0:T(8,128)(4,1)S(1)} %fusion.37, bf16[2048,1,128]{2,0,1:T(8,128)(2,1)S(1)} %get-tuple-element.168, bf16[2048,1,4,128]{0,3,2,1:T(8,128)(2,1)} %get-tuple-element.167, s32[]{:T(128)S(6)} %select_n.40), kind=kOutput, calls=%fused_computation.5.clone.1 | convolution fusion | flops 1086322688 | bytes 18882564 | tf_op jit(solution)/shard_map/while/body/eval_jaxpr/qgrd,kgd->grqk/dot_general | solution.py:38
  79.2 4.5 %fusion.39 = f32[4,512]{1,0:T(4,128)S(1)} fusion(f32[512,4,2048]{2,0,1:T(8,128)S(1)} %get-tuple-element.139, f32[4,512]{1,0:T(4,128)S(1)} %get-tuple-element.140, pred[512,2048]{1,0:T(8,128)(4,1)S(1)} %fusion.37), kind=kLoop, calls=%fused_computation.4.clone.1 | loop fusion | flops 16775168 | bytes 17842176 | tf_op jit(solution)/shard_map/while/body/eval_jaxpr/reduce_sum | solution.py:45
  83.7 5.3 %fusion.40 = bf16[4,512,128]{1,2,0:T(8,128)(2,1)S(1)} fusion(f32[4,512]{1,0:T(4,128)S(1)} %fusion.39, f32[4,512]{1,0:T(4,128)S(1)} %get-tuple-element.140, f32[512,4,2048]{2,0,1:T(8,128)S(1)} %get-tuple-element.139, pred[512,2048]{1,0:T(8,128)(4,1)S(1)} %fusion.37, bf16[2048,1,128]{0,2,1:T(8,128)(2,1)S(1)} %get-tuple-element.169), kind=kOutput, calls=%fused_computation.10.clone.1 | convolution fusion | flops 1094975488 | bytes 18890752 | tf_op jit(solution)/shard_map/while/body/eval_jaxpr/grqk,kgd->qgrd/dot_general | solution.py:46
  89.0 0.2 copy.28
  89.2 0.8 constant_dynamic-update-slice_fusion.2
  90.1 0.6 dynamic_slice.33
  91.4 0.1 dynamic_slice.34
  91.5 1.2 fusion.37
  92.7 4.9 %fusion.38 = (f32[4,512]{1,0:T(4,128)S(1)}, f32[512,4,2048]{2,0,1:T(8,128)S(1)}) fusion(pred[512,2048]{1,0:T(8,128)(4,1)S(1)} %fusion.37, bf16[2048,1,128]{2,0,1:T(8,128)(2,1)S(1)} %get-tuple-element.168, bf16[2048,1,4,128]{0,3,2,1:T(8,128)(2,1)} %get-tuple-element.167, s32[]{:T(128)S(6)} %select_n.40), kind=kOutput, calls=%fused_computation.5.clone.1 | convolution fusion | flops 1086322688 | bytes 18882564 | tf_op jit(solution)/shard_map/while/body/eval_jaxpr/qgrd,kgd->grqk/dot_general | solution.py:38
  97.6 4.5 %fusion.39 = f32[4,512]{1,0:T(4,128)S(1)} fusion(f32[512,4,2048]{2,0,1:T(8,128)S(1)} %get-tuple-element.139, f32[4,512]{1,0:T(4,128)S(1)} %get-tuple-element.140, pred[512,2048]{1,0:T(8,128)(4,1)S(1)} %fusion.37), kind=kLoop, calls=%fused_computation.4.clone.1 | loop fusion | flops 16775168 | bytes 17842176 | tf_op jit(solution)/shard_map/while/body/eval_jaxpr/reduce_sum | solution.py:45
  102.1 5.3 %fusion.40 = bf16[4,512,128]{1,2,0:T(8,128)(2,1)S(1)} fusion(f32[4,512]{1,0:T(4,128)S(1)} %fusion.39, f32[4,512]{1,0:T(4,128)S(1)} %get-tuple-element.140, f32[512,4,2048]{2,0,1:T(8,128)S(1)} %get-tuple-element.139, pred[512,2048]{1,0:T(8,128)(4,1)S(1)} %fusion.37, bf16[2048,1,128]{0,2,1:T(8,128)(2,1)S(1)} %get-tuple-element.169), kind=kOutput, calls=%fused_computation.10.clone.1 | convolution fusion | flops 1094975488 | bytes 18890752 | tf_op jit(solution)/shard_map/while/body/eval_jaxpr/grqk,kgd->qgrd/dot_general | solution.py:46
  107.3 0.2 copy.28
  107.6 0.8 constant_dynamic-update-slice_fusion.2
  108.4 0.6 dynamic_slice.33
  109.7 0.1 dynamic_slice.34
  109.8 1.2 fusion.37
  111.0 4.9 %fusion.38 = (f32[4,512]{1,0:T(4,128)S(1)}, f32[512,4,2048]{2,0,1:T(8,128)S(1)}) fusion(pred[512,2048]{1,0:T(8,128)(4,1)S(1)} %fusion.37, bf16[2048,1,128]{2,0,1:T(8,128)(2,1)S(1)} %get-tuple-element.168, bf16[2048,1,4,128]{0,3,2,1:T(8,128)(2,1)} %get-tuple-element.167, s32[]{:T(128)S(6)} %select_n.40), kind=kOutput, calls=%fused_computation.5.clone.1 | convolution fusion | flops 1086322688 | bytes 18882564 | tf_op jit(solution)/shard_map/while/body/eval_jaxpr/qgrd,kgd->grqk/dot_general | solution.py:38
  115.9 4.5 %fusion.39 = f32[4,512]{1,0:T(4,128)S(1)} fusion(f32[512,4,2048]{2,0,1:T(8,128)S(1)} %get-tuple-element.139, f32[4,512]{1,0:T(4,128)S(1)} %get-tuple-element.140, pred[512,2048]{1,0:T(8,128)(4,1)S(1)} %fusion.37), kind=kLoop, calls=%fused_computation.4.clone.1 | loop fusion | flops 16775168 | bytes 17842176 | tf_op jit(solution)/shard_map/while/body/eval_jaxpr/reduce_sum | solution.py:45
  120.4 5.3 %fusion.40 = bf16[4,512,128]{1,2,0:T(8,128)(2,1)S(1)} fusion(f32[4,512]{1,0:T(4,128)S(1)} %fusion.39, f32[4,512]{1,0:T(4,128)S(1)} %get-tuple-element.140, f32[512,4,2048]{2,0,1:T(8,128)S(1)} %get-tuple-element.139, pred[512,2048]{1,0:T(8,128)(4,1)S(1)} %fusion.37, bf16[2048,1,128]{0,2,1:T(8,128)(2,1)S(1)} %get-tuple-element.169), kind=kOutput, calls=%fused_computation.10.clone.1 | convolution fusion | flops 1094975488 | bytes 18890752 | tf_op jit(solution)/shard_map/while/body/eval_jaxpr/grqk,kgd->qgrd/dot_general | solution.py:46
  125.7 0.2 copy.28
  125.9 0.9 constant_dynamic-update-slice_fusion.2
  126.7 33.7 %all_to_all.13 = bf16[16,128,512]{2,1,0:T(8,128)(2,1)S(1)} all-to-all(bf16[16,128,512]{2,1,0:T(8,128)(2,1)} %bitcast.86), channel_id=1, replica_groups=mesh['dp'=16,'tensor'=16] {'tensor'}, dimensions={0} | all-to-all | bytes 4194304 | tf_op jit(solution)/shard_map/all_to_all | solution.py:67
  160.5 2.5 convert_bitcast_fusion
  163.0 5.3 %copy.20 = f32[128,16,512]{0,2,1:T(8,128)} copy(f32[128,16,512]{2,0,1:T(8,128)} %convert_bitcast_fusion) | data formatting | bytes 8388608 | tf_op jit(solution)/shard_map/convert_element_type | solution.py:68
  168.4 0.5 fusion.18
  168.9 2.9 fusion.20
  171.8 6.3 %fusion.23 = bf16[128,512]{1,0:T(8,128)(2,1)S(1)} fusion(bf16[128,8192]{0,1:T(8,128)(2,1)S(1)} %fusion.20, bf16[8192,512]{0,1:T(8,128)(2,1)} %all-gather.2.cloned.1.call-done, bf16[128,512]{1,0:T(8,128)(2,1)S(1)} %copy-done.2), kind=kOutput, calls=%fused_computation.30 | convolution fusion | flops 1074069504 | bytes 10747904 | tf_op jit(solution)/shard_map/dot_general | solution.py:72
  178.1 8.0 %fusion.24 = f32[8192,512]{1,0:T(8,128)} fusion(bf16[128,8192]{0,1:T(8,128)(2,1)S(1)} %fusion.20, bf16[128,512]{1,0:T(8,128)(2,1)S(1)} %fusion.23), kind=kOutput, calls=%fused_computation.34 | convolution fusion | flops 1073741824 | bytes 19005440 | tf_op jit(solution)/shard_map/dot_general | solution.py:80
  186.2 147.4 %reduce-scatter.5.cloned.1.call-done = f32[512,512]{1,0:T(8,128)} async-done(((f32[8192,512]{1,0:T(8,128)}), f32[512,512]{1,0:T(8,128)}) %reduce-scatter.5.cloned.1.call-update) | async-done | bytes 1048592 | tf_op jit(solution)/shard_map/reduce_scatter | solution.py:79
  333.6 2.5 copy.22
  336.1 71.6 %reduce-scatter.7.cloned.1.call-done = f32[32,512]{1,0:T(8,128)} async-done(((f32[512,512]{1,0:T(8,128)}), f32[32,512]{1,0:T(8,128)}) %reduce-scatter.7.cloned.1.call-update) | async-done | bytes 65552
  (22 shorter events, 0.2 us)
Async XLA Ops:
  6.5 44.3 %copy-start = (bf16[2048,512]{1,0:T(8,128)(2,1)S(1)}, bf16[2048,512]{1,0:T(8,128)(2,1)}, u32[]{:S(2)}) copy-start(bf16[2048,512]{1,0:T(8,128)(2,1)} %param.9) | copy-start | bytes 6291460
  6.5 46.9 %copy-start.1 = (s32[2048]{0:T(1024)S(1)}, s32[2048]{0:T(1024)}, u32[]{:S(2)}) copy-start(s32[2048]{0:T(1024)} %param.12) | copy-start | bytes 24580
  6.5 165.2 %all-gather.2.cloned.1.call-start = ((), (), s32[]{:S(2)}) async-start(), calls=%async_computation.3 | async-start | bytes 8912896 | tf_op jit(solution)/shard_map/all_gather | solution.py:74
  48.4 285.2 %reduce-scatter.5.cloned.1.call-start = ((), (), s32[]{:S(2)}) async-start(), calls=%async_computation.4 | async-start | bytes 17825792 | tf_op jit(solution)/shard_map/reduce_scatter | solution.py:79
  163.0 5.9 %copy-start.3 = (f32[8192]{0:T(1024)S(1)}, f32[8192]{0:T(1024)}, u32[]{:S(2)}) copy-start(f32[8192]{0:T(1024)} %param.13) | copy-start | bytes 98308
  168.4 3.4 copy-start.2
  186.1 221.6 %reduce-scatter.7.cloned.1.call-start = ((), (), s32[]{:S(2)}) async-start(), calls=%async_computation.5 | async-start | bytes 1114112
Sparse Core Ops, SparseCore 0:
  48.5 75.7 all-gather.1
  186.2 147.2 reduce-scatter.4
  336.3 71.4 reduce-scatter.6
where the time goes:
time: 415 us; the launch traced here: 414 us
  waiting for transfers between devices  219 us (53%)
  blocking collectives  75.5 us (18%)
  matrix products  55 us (13%)
  other arithmetic  28.6 us (7%)
  local copies, waits for them, and re-layouts  20 us (5%)
  between operations  13.2 us (3%)
    reduce_scatter x1, waiting for transfers between devices, on_device(): lax.psum_scatter(lax.dot_general(picked, grad_pred, (((0,), (0,)), ((), (...  147 us
    unnamed x4, waiting for transfers between devices  71.7 us
    all_gather x1, blocking collectives, on_device(): weight_slab = lax.all_gather(draft_weight, 'dp', axis=1, tiled=True)  41.8 us
    all_to_all x1, blocking collectives, on_device(): lax.all_to_all(attended, 'tensor', split_axis=0, concat_axis=1, tiled=True)  33.7 us
    dot_general x4, matrix products, one_block(): jnp.einsum('grqk,kgd->qgrd', probs, values_local, preferred_element_type=...  21.1 us
    dot_general x4, matrix products, one_block(): jnp.einsum('qgrd,kgd->grqk', query_block, keys_local, preferred_element_t...  19.5 us
    reduce_sum x4, other arithmetic, one_block(): jnp.sum(shifted, axis=-1, keepdims=True)  17.9 us
  transfers between devices with their start and end apart: 3, of which 2 were waited for; matrix products, arithmetic and copies ran while one was open for 21% of the time, Pallas kernels for 0%

commit v1 on v0

--- a/solution.py
+++ b/solution.py
@@ -64,7 +64,10 @@
     length = query_rows.shape[0]
     total_tokens = length * lax.axis_size("dp")
     weight_slab = lax.all_gather(draft_weight, "dp", axis=1, tiled=True)
-    regrouped = lax.all_to_all(attended, "tensor", split_axis=0, concat_axis=1, tiled=True)
+    devices = lax.axis_size("tensor")
+    blocks = jnp.stack(jnp.split(attended, devices, axis=0), axis=0)
+    blocks = lax.all_to_all(blocks, "tensor", split_axis=0, concat_axis=0)
+    regrouped = jnp.concatenate(blocks, axis=1)
     features = regrouped.astype(jnp.float32)
     mean_square = jnp.mean(features * features, axis=-1, keepdims=True)
     normed = (features * lax.rsqrt(mean_square + 1e-06) * norm_gain[None, :]).astype(jnp.bfloat16)

time: 415 us -> 420 us (1.012)
  matrix products: 55 us -> 60 us
    dot_general x4, matrix products: 21.1 us -> 25.3 us  [one_block(): jnp.einsum('grqk,kgd->qgrd', probs, values_local, preferred_element_type=...]
  transfers between devices with their start and end apart: 3 -> 3, of which waited for: 2 -> 2; matrix products, arithmetic and copies ran while one was open for 21% -> 22% of each run, Pallas kernels for 0% -> 0%
where the time goes in v1:
time: 420 us; the launch traced here: 419 us
  waiting for transfers between devices  219 us (52%)
  blocking collectives  75.2 us (18%)
  matrix products  60 us (14%)
  other arithmetic  28.6 us (7%)
  local copies, waits for them, and re-layouts  20.1 us (5%)
  between operations  13.3 us (3%)
    reduce_scatter x1, waiting for transfers between devices, on_device(): lax.psum_scatter(lax.dot_general(picked, grad_pred, (((0,), (0,)), ((), (...  147 us
    unnamed x4, waiting for transfers between devices  71.8 us
    all_gather x1, blocking collectives, on_device(): weight_slab = lax.all_gather(draft_weight, 'dp', axis=1, tiled=True)  41.7 us
    all_to_all x1, blocking collectives, on_device(): blocks = lax.all_to_all(blocks, 'tensor', split_axis=0, concat_axis=0)  33.5 us
    dot_general x4, matrix products, one_block(): jnp.einsum('grqk,kgd->qgrd', probs, values_local, preferred_element_type=...  25.3 us
    dot_general x4, matrix products, one_block(): jnp.einsum('qgrd,kgd->grqk', query_block, keys_local, preferred_element_t...  20.3 us
    reduce_sum x4, other arithmetic, one_block(): jnp.sum(shifted, axis=-1, keepdims=True)  17.9 us
  transfers between devices with their start and end apart: 3, of which 2 were waited for; matrix products, arithmetic and copies ran while one was open for 22% of the time, Pallas kernels for 0%

profile of v1, /device:TPU:8, one launch (start us, length us, event | category | flops | bytes accessed | tf_op | source)
XLA Modules:
  0.0 419.2 jit_solution(14437266836451340016)
XLA Ops:
  6.5 41.7 %all_gather.6 = bf16[512,512]{0,1:T(8,128)(2,1)} all-gather(bf16[512,32]{0,1:T(8,128)(2,1)} %param.14), channel_id=1, replica_groups=mesh['dp'=16,'tensor'=16] {'dp'}, dimensions={1}, use_global_device_ids=true | all-gather | bytes 557056 | tf_op jit(solution)/shard_map/all_gather | solution.py:66
  48.2 0.0 reduce-scatter.5.cloned.1.call-start
  48.3 1.1 constant_dynamic-slice_fusion
  49.4 1.0 copy.17
  50.4 1.9 dynamic-slice_bitcast_fusion
  52.3 4.0 copy.16
  56.3 74.8 %while.11 = (s32[]{:T(128)}, bf16[4,512,512]{2,1,0:T(8,128)(2,1)S(1)}, s32[4]{0:T(128)S(1)}, s32[2048]{0:T(1024)S(1)}, bf16[2048,1,4,128]{0,3,2,1:T(8,128)(2,1)}...) while((s32[]{:T(128)}, ...), condition=%wide.region_3.4_spmd.clone, body=%wide.region_0.3_spmd.clone.sunk | while | flops 2201219584 | bytes 58779828 | solution.py:51
  56.3 0.6 dynamic_slice.33
  57.6 0.1 dynamic_slice.34
  57.6 1.2 fusion.53
  58.8 5.1 %fusion.54 = (f32[4,512]{1,0:T(4,128)S(1)}, f32[512,4,2048]{2,0,1:T(8,128)S(1)}) fusion(pred[512,2048]{1,0:T(8,128)(4,1)S(1)} %fusion.53, bf16[2048,1,128]{2,0,1:T(8,128)(2,1)} %get-tuple-element.168, bf16[2048,1,4,128]{0,3,2,1:T(8,128)(2,1)} %get-tuple-element.167, s32[]{:T(128)S(6)} %select_n.40), kind=kOutput, calls=%fused_computation.5.clone.1 | convolution fusion | flops 1086322688 | bytes 18882564 | tf_op jit(solution)/shard_map/while/body/eval_jaxpr/qgrd,kgd->grqk/dot_general | solution.py:38
  63.9 4.5 %fusion.55 = f32[4,512]{1,0:T(4,128)S(1)} fusion(f32[512,4,2048]{2,0,1:T(8,128)S(1)} %get-tuple-element.139, f32[4,512]{1,0:T(4,128)S(1)} %get-tuple-element.140, pred[512,2048]{1,0:T(8,128)(4,1)S(1)} %fusion.53), kind=kLoop, calls=%fused_computation.4.clone.1 | loop fusion | flops 16775168 | bytes 17842176 | tf_op jit(solution)/shard_map/while/body/eval_jaxpr/reduce_sum | solution.py:45
  68.4 6.3 %fusion.56 = bf16[4,512,128]{1,2,0:T(8,128)(2,1)S(1)} fusion(f32[4,512]{1,0:T(4,128)S(1)} %fusion.55, f32[4,512]{1,0:T(4,128)S(1)} %get-tuple-element.140, f32[512,4,2048]{2,0,1:T(8,128)S(1)} %get-tuple-element.139, pred[512,2048]{1,0:T(8,128)(4,1)S(1)} %fusion.53, bf16[2048,1,128]{0,2,1:T(8,128)(2,1)} %get-tuple-element.169), kind=kOutput, calls=%fused_computation.10.clone.1 | convolution fusion | flops 1094975488 | bytes 18890752 | tf_op jit(solution)/shard_map/while/body/eval_jaxpr/grqk,kgd->qgrd/dot_general | solution.py:46
  74.7 0.2 copy.28
  75.0 0.6 dynamic_slice.33
  76.3 0.1 dynamic_slice.34
  76.3 1.2 fusion.53
  77.5 5.1 %fusion.54 = (f32[4,512]{1,0:T(4,128)S(1)}, f32[512,4,2048]{2,0,1:T(8,128)S(1)}) fusion(pred[512,2048]{1,0:T(8,128)(4,1)S(1)} %fusion.53, bf16[2048,1,128]{2,0,1:T(8,128)(2,1)} %get-tuple-element.168, bf16[2048,1,4,128]{0,3,2,1:T(8,128)(2,1)} %get-tuple-element.167, s32[]{:T(128)S(6)} %select_n.40), kind=kOutput, calls=%fused_computation.5.clone.1 | convolution fusion | flops 1086322688 | bytes 18882564 | tf_op jit(solution)/shard_map/while/body/eval_jaxpr/qgrd,kgd->grqk/dot_general | solution.py:38
  82.6 4.5 %fusion.55 = f32[4,512]{1,0:T(4,128)S(1)} fusion(f32[512,4,2048]{2,0,1:T(8,128)S(1)} %get-tuple-element.139, f32[4,512]{1,0:T(4,128)S(1)} %get-tuple-element.140, pred[512,2048]{1,0:T(8,128)(4,1)S(1)} %fusion.53), kind=kLoop, calls=%fused_computation.4.clone.1 | loop fusion | flops 16775168 | bytes 17842176 | tf_op jit(solution)/shard_map/while/body/eval_jaxpr/reduce_sum | solution.py:45
  87.1 6.3 %fusion.56 = bf16[4,512,128]{1,2,0:T(8,128)(2,1)S(1)} fusion(f32[4,512]{1,0:T(4,128)S(1)} %fusion.55, f32[4,512]{1,0:T(4,128)S(1)} %get-tuple-element.140, f32[512,4,2048]{2,0,1:T(8,128)S(1)} %get-tuple-element.139, pred[512,2048]{1,0:T(8,128)(4,1)S(1)} %fusion.53, bf16[2048,1,128]{0,2,1:T(8,128)(2,1)} %get-tuple-element.169), kind=kOutput, calls=%fused_computation.10.clone.1 | convolution fusion | flops 1094975488 | bytes 18890752 | tf_op jit(solution)/shard_map/while/body/eval_jaxpr/grqk,kgd->qgrd/dot_general | solution.py:46
  93.5 0.2 copy.28
  93.7 0.6 dynamic_slice.33
  95.0 0.1 dynamic_slice.34
  95.0 1.2 fusion.53
  96.2 5.1 %fusion.54 = (f32[4,512]{1,0:T(4,128)S(1)}, f32[512,4,2048]{2,0,1:T(8,128)S(1)}) fusion(pred[512,2048]{1,0:T(8,128)(4,1)S(1)} %fusion.53, bf16[2048,1,128]{2,0,1:T(8,128)(2,1)} %get-tuple-element.168, bf16[2048,1,4,128]{0,3,2,1:T(8,128)(2,1)} %get-tuple-element.167, s32[]{:T(128)S(6)} %select_n.40), kind=kOutput, calls=%fused_computation.5.clone.1 | convolution fusion | flops 1086322688 | bytes 18882564 | tf_op jit(solution)/shard_map/while/body/eval_jaxpr/qgrd,kgd->grqk/dot_general | solution.py:38
  101.3 4.5 %fusion.55 = f32[4,512]{1,0:T(4,128)S(1)} fusion(f32[512,4,2048]{2,0,1:T(8,128)S(1)} %get-tuple-element.139, f32[4,512]{1,0:T(4,128)S(1)} %get-tuple-element.140, pred[512,2048]{1,0:T(8,128)(4,1)S(1)} %fusion.53), kind=kLoop, calls=%fused_computation.4.clone.1 | loop fusion | flops 16775168 | bytes 17842176 | tf_op jit(solution)/shard_map/while/body/eval_jaxpr/reduce_sum | solution.py:45
  105.8 6.3 %fusion.56 = bf16[4,512,128]{1,2,0:T(8,128)(2,1)S(1)} fusion(f32[4,512]{1,0:T(4,128)S(1)} %fusion.55, f32[4,512]{1,0:T(4,128)S(1)} %get-tuple-element.140, f32[512,4,2048]{2,0,1:T(8,128)S(1)} %get-tuple-element.139, pred[512,2048]{1,0:T(8,128)(4,1)S(1)} %fusion.53, bf16[2048,1,128]{0,2,1:T(8,128)(2,1)} %get-tuple-element.169), kind=kOutput, calls=%fused_computation.10.clone.1 | convolution fusion | flops 1094975488 | bytes 18890752 | tf_op jit(solution)/shard_map/while/body/eval_jaxpr/grqk,kgd->qgrd/dot_general | solution.py:46
  112.2 0.2 copy.28
  112.4 0.6 dynamic_slice.33
  113.7 0.1 dynamic_slice.34
  113.7 1.2 fusion.53
  114.9 5.1 %fusion.54 = (f32[4,512]{1,0:T(4,128)S(1)}, f32[512,4,2048]{2,0,1:T(8,128)S(1)}) fusion(pred[512,2048]{1,0:T(8,128)(4,1)S(1)} %fusion.53, bf16[2048,1,128]{2,0,1:T(8,128)(2,1)} %get-tuple-element.168, bf16[2048,1,4,128]{0,3,2,1:T(8,128)(2,1)} %get-tuple-element.167, s32[]{:T(128)S(6)} %select_n.40), kind=kOutput, calls=%fused_computation.5.clone.1 | convolution fusion | flops 1086322688 | bytes 18882564 | tf_op jit(solution)/shard_map/while/body/eval_jaxpr/qgrd,kgd->grqk/dot_general | solution.py:38
  120.0 4.5 %fusion.55 = f32[4,512]{1,0:T(4,128)S(1)} fusion(f32[512,4,2048]{2,0,1:T(8,128)S(1)} %get-tuple-element.139, f32[4,512]{1,0:T(4,128)S(1)} %get-tuple-element.140, pred[512,2048]{1,0:T(8,128)(4,1)S(1)} %fusion.53), kind=kLoop, calls=%fused_computation.4.clone.1 | loop fusion | flops 16775168 | bytes 17842176 | tf_op jit(solution)/shard_map/while/body/eval_jaxpr/reduce_sum | solution.py:45
  124.5 6.3 %fusion.56 = bf16[4,512,128]{1,2,0:T(8,128)(2,1)S(1)} fusion(f32[4,512]{1,0:T(4,128)S(1)} %fusion.55, f32[4,512]{1,0:T(4,128)S(1)} %get-tuple-element.140, f32[512,4,2048]{2,0,1:T(8,128)S(1)} %get-tuple-element.139, pred[512,2048]{1,0:T(8,128)(4,1)S(1)} %fusion.53, bf16[2048,1,128]{0,2,1:T(8,128)(2,1)} %get-tuple-element.169), kind=kOutput, calls=%fused_computation.10.clone.1 | convolution fusion | flops 1094975488 | bytes 18890752 | tf_op jit(solution)/shard_map/while/body/eval_jaxpr/grqk,kgd->qgrd/dot_general | solution.py:46
  130.9 0.2 copy.28
  131.4 33.5 %all_to_all.5 = bf16[16,128,512]{2,1,0:T(8,128)(2,1)S(1)} all-to-all(bf16[16,128,512]{2,1,0:T(8,128)(2,1)S(1)} %fusion.24), channel_id=1, replica_groups=mesh['dp'=16,'tensor'=16] {'tensor'}, dimensions={0} | all-to-all | bytes 4194304 | tf_op jit(solution)/shard_map/all_to_all | solution.py:69
  165.0 2.5 convert_bitcast_fusion
  167.5 5.3 %copy.20 = f32[128,16,512]{0,2,1:T(8,128)} copy(f32[128,16,512]{2,0,1:T(8,128)} %convert_bitcast_fusion) | data formatting | bytes 8388608 | tf_op jit(solution)/shard_map/convert_element_type | solution.py:71
  172.9 0.5 fusion.18
  173.4 0.3 copy-done.2
  173.6 2.9 fusion.20
  176.5 0.0 all-gather.2.cloned.1.call-done
  176.5 6.3 %fusion.23 = bf16[128,512]{1,0:T(8,128)(2,1)S(1)} fusion(bf16[128,8192]{0,1:T(8,128)(2,1)S(1)} %fusion.20, bf16[8192,512]{0,1:T(8,128)(2,1)} %all-gather.2.cloned.1.call-done, bf16[128,512]{1,0:T(8,128)(2,1)S(1)} %copy-done.1), kind=kOutput, calls=%fused_computation.30 | convolution fusion | flops 1074069504 | bytes 10747904 | tf_op jit(solution)/shard_map/dot_general | solution.py:75
  182.8 8.0 %fusion.40 = f32[8192,512]{1,0:T(8,128)} fusion(bf16[128,8192]{0,1:T(8,128)(2,1)S(1)} %fusion.20, bf16[128,512]{1,0:T(8,128)(2,1)S(1)} %fusion.23), kind=kOutput, calls=%fused_computation.66 | convolution fusion | flops 1073741824 | bytes 19005440 | tf_op jit(solution)/shard_map/dot_general | solution.py:83
  190.9 0.0 reduce-scatter.7.cloned.1.call-start
  191.0 147.5 %reduce-scatter.5.cloned.1.call-done = f32[512,512]{1,0:T(8,128)} async-done(((f32[8192,512]{1,0:T(8,128)}), f32[512,512]{1,0:T(8,128)}) %reduce-scatter.5.cloned.1.call-update) | async-done | bytes 1048592 | tf_op jit(solution)/shard_map/reduce_scatter | solution.py:82
  338.4 2.5 copy.22
  341.0 71.7 %reduce-scatter.7.cloned.1.call-done = f32[32,512]{1,0:T(8,128)} async-done(((f32[512,512]{1,0:T(8,128)}), f32[32,512]{1,0:T(8,128)}) %reduce-scatter.7.cloned.1.call-update) | async-done | bytes 65552
  (36 shorter events, 0.4 us)
Async XLA Ops:
  6.5 170.0 %all-gather.2.cloned.1.call-start = ((), (), s32[]{:S(2)}) async-start(), calls=%async_computation.3 | async-start | bytes 8912896 | tf_op jit(solution)/shard_map/all_gather | solution.py:77
  48.2 290.2 %reduce-scatter.5.cloned.1.call-start = ((), (), s32[]{:S(2)}) async-start(), calls=%async_computation.4 | async-start | bytes 17825792 | tf_op jit(solution)/shard_map/reduce_scatter | solution.py:82
  52.3 4.0 copy-start
  172.9 0.8 copy-start.2
  173.6 2.9 copy-start.1
  190.9 221.8 %reduce-scatter.7.cloned.1.call-start = ((), (), s32[]{:S(2)}) async-start(), calls=%async_computation.5 | async-start | bytes 1114112
Sparse Core Ops, SparseCore 0:
  48.4 75.7 all-gather.1
  191.0 147.3 reduce-scatter.4
  341.1 71.5 reduce-scatter.6
